TPU v7x, 256 devices: a whole 4x4x8 slice. The times are simulated.
256 devices in a mesh: section: 2 (over core), seq: 16 (over y, x), mp: 8 (over z).
Axes of the slice: x: 4, y: 4, z: 8, core: 2. Of those that a mesh axis runs over, the one named last changes fastest.
Arguments:
- stream: bfloat16 [2, 2048, 3584], P(None, 'seq', 'mp'), may hold values from -6 to 6
- segment_ids: int32 [2, 2048], P(None, 'seq'), may hold values from 0 to 1, never falling along the last dimension, each value on 1 to 1536 neighbouring positions
- norm_gain: bfloat16 [2, 3584], P('section'), may hold values from 0.5 to 1.5
- in_weight: bfloat16 [2, 3584, 2, 4096], P('section', None, None, 'mp'), may hold values from -0.09375 to 0.09375
- bc_weight: bfloat16 [2, 3584, 128], P('section'), may hold values from -0.09375 to 0.09375
- dt_weight: bfloat16 [2, 3584, 64], P('section', None, 'mp'), may hold values from -0.09375 to 0.09375
- dt_bias: float32 [2, 64], P('section', 'mp'), may hold values from -4 to -1
- decay_rate: float32 [2, 64], P('section', 'mp'), may hold values from 0.001 to 0.5
- conv_inner: float32 [2, 4, 4096], P('section', None, 'mp'), may hold values from -3 to 3
- conv_state: float32 [2, 4, 128], P('section'), may hold values from -3 to 3
- skip_gain: float32 [2, 64], P('section', 'mp'), may hold values from 0.5 to 1.5
- inner_gain: bfloat16 [2, 4096], P('section', 'mp'), may hold values from 0.5 to 1.5
- out_weight: bfloat16 [2, 4096, 3584], P('section', 'mp'), may hold values from -0.09375 to 0.09375
Outputs:
- hidden: bfloat16 [2, 2, 2048, 3584], P('section', None, 'seq', 'mp')
Inputs may be any that keep to these rules, and one draw needn't show every extreme that they name: `segment_ids`: within each micro-batch the document numbers start at 0 and rise by one at each new document; a document has 1 to 1536 positions.
All inputs are finite; a program needn't handle non-finite values.
Results may differ from a plain program's by a relative error of at most 0.023.
Values may be sent and summed in bfloat16 or wider, within the bound.
A program may use at most 128 MiB of HBM per device.

v0:
```python
import jax
import jax.numpy as jnp
from jax import lax
from jax.sharding import PartitionSpec as P

HDIM = 64
STATE = 64
INNER = 4096
EPS = 1e-05


def shifted(block, axis, distance):
    devices = range(lax.axis_size(axis))
    route = [(i - distance, i) for i in devices if i - distance in devices]
    return lax.ppermute(block, axis, route)


def norm_rows(hidden_rows, gain):
    values = hidden_rows.astype(jnp.float32)
    scale = lax.rsqrt(jnp.mean(values * values, axis=-1, keepdims=True) + EPS)
    return (values * scale * gain.astype(jnp.float32)).astype(jnp.bfloat16)


def causal_conv(padded, pad_docs, documents, taps):
    length = documents.shape[0]
    total = jnp.zeros((length, padded.shape[1]), jnp.float32)
    for offset in range(taps.shape[0]):
        match = (pad_docs[offset : offset + length] == documents)[:, None]
        term = padded[offset : offset + length].astype(jnp.float32) * taps[offset][None, :]
        total = total + jnp.where(match, term, 0.0)
    return jax.nn.silu(total).astype(jnp.bfloat16)


def block_terms(inputs, b_rows, c_rows, steps_dt, documents, prior_doc, decay_rate):
    length = documents.shape[0]
    cumlog = jnp.cumsum(-steps_dt * decay_rate[None, :], axis=0)
    places = jnp.arange(length, dtype=jnp.int32)
    same_doc = (documents[:, None] == documents[None, :]) & (places[:, None] >= places[None, :])
    gap_log = jnp.where(same_doc[:, :, None], cumlog[:, None, :] - cumlog[None, :, :], 0.0)
    decays = jnp.where(same_doc[:, :, None], jnp.exp(gap_log), 0.0)
    intersection = jnp.dot(c_rows, b_rows.T, preferred_element_type=jnp.float32)
    mixing = (decays * intersection[:, :, None] * steps_dt[None, :, :]).astype(jnp.bfloat16)
    local_out = jnp.einsum("tsh,shp->thp", mixing, inputs, preferred_element_type=jnp.float32)
    carry_in = jnp.where((documents == prior_doc)[:, None], jnp.exp(cumlog), 0.0)
    last_doc = documents[-1]
    tail_weight = (
        jnp.where((documents == last_doc)[:, None], jnp.exp(cumlog[-1][None, :] - cumlog), 0.0)
        * steps_dt
    )
    local_state = jnp.einsum(
        "sh,shp,sn->hpn",
        tail_weight,
        inputs.astype(jnp.float32),
        b_rows.astype(jnp.float32),
        precision=lax.Precision.HIGHEST,
    )
    through = jnp.where(last_doc == prior_doc, jnp.exp(cumlog[-1]), 0.0)
    return (local_out, carry_in, local_state, through)


def mixer_layer(
    hidden_rows,
    documents,
    norm_gain,
    in_weight,
    bc_weight,
    dt_weight,
    dt_bias,
    decay_rate,
    conv_inner,
    conv_state,
    skip_gain,
    inner_gain,
    out_weight,
):
    whole = lax.all_gather(hidden_rows, "mp", axis=1, tiled=True)
    normed = norm_rows(whole, norm_gain)
    width_loc = in_weight.shape[-1]
    both = jnp.dot(
        normed, in_weight.reshape(in_weight.shape[0], -1), preferred_element_type=jnp.float32
    )
    inner_raw = both[:, :width_loc]
    gate_raw = both[:, width_loc:]
    state_raw = jnp.dot(normed, bc_weight, preferred_element_type=jnp.float32)
    dt_raw = jnp.dot(normed, dt_weight, preferred_element_type=jnp.float32)
    joined = jnp.concatenate([inner_raw, state_raw], axis=1).astype(jnp.bfloat16)
    taps = jnp.concatenate([conv_inner, conv_state], axis=1)
    lag = taps.shape[0] - 1
    rim_rows, rim_docs = shifted((joined[-lag:], documents[-lag:]), "seq", 1)
    padded = jnp.concatenate([rim_rows, joined], axis=0)
    pad_docs = jnp.concatenate([rim_docs, documents], axis=0)
    mixed_in = causal_conv(padded, pad_docs, documents, taps)
    length = documents.shape[0]
    heads = width_loc // HDIM
    inputs = mixed_in[:, :width_loc].reshape(length, heads, HDIM)
    b_rows = mixed_in[:, width_loc : width_loc + STATE]
    c_rows = mixed_in[:, width_loc + STATE :]
    steps_dt = jax.nn.softplus(dt_raw + dt_bias[None, :])
    local_out, carry_in, local_state, through = block_terms(
        inputs, b_rows, c_rows, steps_dt, documents, rim_docs[-1], decay_rate
    )

    def relay(turn_index, state_in):
        return shifted(
            (through[:, None, None] * state_in + local_state).astype(jnp.bfloat16), "seq", 1
        ).astype(jnp.float32)

    state_in = lax.fori_loop(0, lax.axis_size("seq") - 1, relay, jnp.zeros_like(local_state))
    from_state = jnp.einsum(
        "tn,hpn->thp", c_rows.astype(jnp.float32), state_in, precision=lax.Precision.HIGHEST
    )
    results = (
        local_out
        + carry_in[:, :, None] * from_state
        + skip_gain[None, :, None] * inputs.astype(jnp.float32)
    )
    gated = results.reshape(length, width_loc) * jax.nn.silu(gate_raw)
    squares = lax.psum(jnp.sum(gated * gated, axis=-1), "mp")
    scale = lax.rsqrt(squares / INNER + EPS)
    normed_inner = (gated * scale[:, None] * inner_gain.astype(jnp.float32)).astype(jnp.bfloat16)
    update = jnp.dot(normed_inner, out_weight, preferred_element_type=jnp.float32)
    summed = lax.psum_scatter(
        update.astype(jnp.bfloat16), "mp", scatter_dimension=1, tiled=True
    ).astype(jnp.float32)
    return (hidden_rows.astype(jnp.float32) + summed).astype(jnp.bfloat16)


def per_device(
    stream,
    segment_ids,
    norm_gain,
    in_weight,
    bc_weight,
    dt_weight,
    dt_bias,
    decay_rate,
    conv_inner,
    conv_state,
    skip_gain,
    inner_gain,
    out_weight,
):
    first = lax.axis_index("section") == 0
    count = stream.shape[0]
    out_layer = out_weight[0]
    received = jnp.zeros_like(stream[0])
    outputs = []
    for step_index in range(count + 1):
        own_rows = stream[min(step_index, count - 1)]
        own_docs = jnp.where(
            first, segment_ids[min(step_index, count - 1)], segment_ids[max(step_index - 1, 0)]
        )
        layer_in = jnp.where(first, own_rows, received)
        result = mixer_layer(
            layer_in,
            own_docs,
            norm_gain[0],
            in_weight[0],
            bc_weight[0],
            dt_weight[0],
            dt_bias[0],
            decay_rate[0],
            conv_inner[0],
            conv_state[0],
            skip_gain[0],
            inner_gain[0],
            out_layer,
        )
        outputs.append(result)
        if step_index < count:
            received = shifted(result, "section", 1)
    final = jnp.stack(
        [
            jnp.where(first, outputs[index_micro], outputs[index_micro + 1])
            for index_micro in range(count)
        ]
    )
    return final[None]


def solution(mesh):
    placed = (
        P(None, "seq", "mp"),
        P(None, "seq"),
        P("section", None),
        P("section", None, None, "mp"),
        P("section", None, None),
        P("section", None, "mp"),
        P("section", "mp"),
        P("section", "mp"),
        P("section", None, "mp"),
        P("section", None, None),
        P("section", "mp"),
        P("section", "mp"),
        P("section", "mp", None),
    )
    return jax.shard_map(
        per_device,
        mesh=mesh,
        in_specs=placed,
        out_specs=P("section", None, "seq", "mp"),
        check_vma=False,
    )
```

profile of v0, /device:TPU:2, one launch (start us, length us, event | category | flops | bytes accessed | tf_op | source)
XLA Modules:
  0.0 758.4 jit_solution(8213100159065672628)
XLA Ops:
  7.5 30.2 %all-gather = bf16[1,128,3584]{1,2,0:T(8,128)(2,1)S(1)} all-gather(bf16[1,128,448]{1,2,0:T(8,128)(2,1)S(1)} %slice_select_fusion), channel_id=2, replica_groups=mesh['section'=2,'seq'=16,'mp'=8] {'mp'}, dimensions={2}, use_global_device_ids=true | all-gather | bytes 1032192 | tf_op jit(solution)/shard_map/all_gather | solution.py:76
  66.2 130.9 %while.33 = (s32[]{:T(128)}, f32[8,64,64]{2,1,0:T(8,128)S(1)}, f32[8]{0:T(128)S(1)}, f32[8,64,64]{2,1,0:T(8,128)S(1)}, s32[]{:T(128)}, /*index=5*/s32[]{:T(128)}) while((s32[]{:T(128)}, f32[8,64,64]{2,1,0:T(8,128)S(1)}, f32[8]{0:T(128)S(1)}, f32[8,64,64]{2,1,0:T(8,128)S(1)}, s32[]{:T(128)}, /*index=5*/s32[]{:T(128)}) %tuple.86), condition=%wide.region_3.4_spmd.clone, body=%wide.region_2.3_spmd.clone.sunk | while | flops 163843 | bytes 786583 | solution.py:108
  95.2 6.5 collective-permute-start
  104.4 6.5 collective-permute-start
  113.5 6.5 collective-permute-start
  122.6 6.5 collective-permute-start
  132.0 6.8 collective-permute-start
  142.7 6.4 collective-permute-start
  152.0 6.0 collective-permute-start
  160.7 6.5 collective-permute-start
  169.8 6.5 collective-permute-start
  178.9 6.5 collective-permute-start
  188.1 6.5 collective-permute-start
  197.7 16.1 %psum.21 = f32[128]{0:T(128)S(1)} all-reduce(f32[128]{0:T(128)S(1)} %multiply_reduce_fusion.2), channel_id=1, replica_groups=mesh['section'=2,'seq'=16,'mp'=8] {'mp'}, use_global_device_ids=true, to_apply=%region_5.6 | all-reduce | flops 128 | bytes 1024 | tf_op jit(solution)/shard_map/psum | solution.py:118
  218.6 6.4 collective-permute-start.6
  228.2 34.4 %reduce-scatter.4.cloned.1.call-done = bf16[128,448]{0,1:T(8,128)(2,1)} async-done(((bf16[128,3584]{0,1:T(8,128)(2,1)}), bf16[128,448]{0,1:T(8,128)(2,1)}) %reduce-scatter.4.cloned.1.call-update) | async-done | bytes 114704 | tf_op jit(solution)/shard_map/reduce_scatter | solution.py:122
  266.1 26.7 %all_gather.10 = bf16[128,3584]{0,1:T(8,128)(2,1)S(1)} all-gather(bf16[128,448]{0,1:T(8,128)(2,1)S(1)} %bitcast_select_fusion.1), channel_id=1, replica_groups=mesh['section'=2,'seq'=16,'mp'=8] {'mp'}, dimensions={1}, use_global_device_ids=true | all-gather | bytes 1032192 | tf_op jit(solution)/shard_map/all_gather | solution.py:76
  307.4 132.7 %while.34 = (s32[]{:T(128)}, f32[8,64,64]{2,1,0:T(8,128)S(1)}, f32[8]{0:T(128)S(1)}, f32[8,64,64]{2,1,0:T(8,128)S(1)}, s32[]{:T(128)}, /*index=5*/s32[]{:T(128)}) while((s32[]{:T(128)}, f32[8,64,64]{2,1,0:T(8,128)S(1)}, f32[8]{0:T(128)S(1)}, f32[8,64,64]{2,1,0:T(8,128)S(1)}, s32[]{:T(128)}, /*index=5*/s32[]{:T(128)}) %tuple.89), condition=%wide.region_10.11_spmd.clone, body=%wide.region_9.10_spmd.clone.sunk | while | flops 163843 | bytes 786583 | solution.py:108
  329.3 6.3 collective-permute-start.1
  338.2 6.5 collective-permute-start.1
  347.4 6.5 collective-permute-start.1
  356.5 6.5 collective-permute-start.1
  365.6 6.5 collective-permute-start.1
  375.0 6.8 collective-permute-start.1
  385.7 6.4 collective-permute-start.1
  395.0 6.0 collective-permute-start.1
  403.7 6.5 collective-permute-start.1
  412.9 6.5 collective-permute-start.1
  422.0 6.5 collective-permute-start.1
  431.1 6.5 collective-permute-start.1
  440.8 15.9 %psum.22 = f32[128]{0:T(128)S(1)} all-reduce(f32[128]{0:T(128)S(1)} %multiply_reduce_fusion.1), channel_id=1, replica_groups=mesh['section'=2,'seq'=16,'mp'=8] {'mp'}, use_global_device_ids=true, to_apply=%region_12.13 | all-reduce | flops 128 | bytes 1024 | tf_op jit(solution)/shard_map/psum | solution.py:118
  461.3 45.0 %reduce-scatter.6.cloned.1.call-done = bf16[128,448]{0,1:T(8,128)(2,1)} async-done(((bf16[128,3584]{0,1:T(8,128)(2,1)}), bf16[128,448]{0,1:T(8,128)(2,1)}) %reduce-scatter.6.cloned.1.call-update) | async-done | bytes 114704 | tf_op jit(solution)/shard_map/reduce_scatter | solution.py:122
  510.0 26.5 %all_gather.11 = bf16[128,3584]{0,1:T(8,128)(2,1)S(1)} all-gather(bf16[128,448]{0,1:T(8,128)(2,1)S(1)} %bitcast_select_fusion), channel_id=1, replica_groups=mesh['section'=2,'seq'=16,'mp'=8] {'mp'}, dimensions={1}, use_global_device_ids=true | all-gather | bytes 1032192 | tf_op jit(solution)/shard_map/all_gather | solution.py:76
  551.0 132.5 %while.35 = (s32[]{:T(128)}, f32[8,64,64]{2,1,0:T(8,128)S(1)}, f32[8]{0:T(128)S(1)}, f32[8,64,64]{2,1,0:T(8,128)S(1)}, s32[]{:T(128)}, /*index=5*/s32[]{:T(128)}) while((s32[]{:T(128)}, f32[8,64,64]{2,1,0:T(8,128)S(1)}, f32[8]{0:T(128)S(1)}, f32[8,64,64]{2,1,0:T(8,128)S(1)}, s32[]{:T(128)}, /*index=5*/s32[]{:T(128)}) %tuple.92), condition=%wide.region_17.18_spmd.clone, body=%wide.region_16.17_spmd.clone.sunk | while | flops 163843 | bytes 786583 | solution.py:108
  572.6 6.5 collective-permute-start.2
  581.7 6.5 collective-permute-start.2
  590.9 6.5 collective-permute-start.2
  600.0 6.5 collective-permute-start.2
  609.1 6.5 collective-permute-start.2
  618.6 6.8 collective-permute-start.2
  629.2 6.5 collective-permute-start.2
  638.3 6.2 collective-permute-start.2
  647.2 6.5 collective-permute-start.2
  656.3 6.5 collective-permute-start.2
  665.4 6.5 collective-permute-start.2
  674.6 6.5 collective-permute-start.2
  684.2 16.1 %psum.23 = f32[128]{0:T(128)S(1)} all-reduce(f32[128]{0:T(128)S(1)} %multiply_reduce_fusion), channel_id=1, replica_groups=mesh['section'=2,'seq'=16,'mp'=8] {'mp'}, use_global_device_ids=true, to_apply=%region_19.20 | all-reduce | flops 128 | bytes 1024 | tf_op jit(solution)/shard_map/psum | solution.py:118
  704.9 45.3 %reduce-scatter.8.cloned.1.call-done = bf16[128,448]{0,1:T(8,128)(2,1)} async-done(((bf16[128,3584]{0,1:T(8,128)(2,1)}), bf16[128,448]{0,1:T(8,128)(2,1)}) %reduce-scatter.8.cloned.1.call-update) | async-done | bytes 114704 | tf_op jit(solution)/shard_map/reduce_scatter | solution.py:122
  (299 shorter events, 250.8 us)
Async XLA Ops:
  6.5 256.1 %reduce-scatter.4.cloned.1.call-start = ((), (), s32[]{:S(2)}) async-start(), calls=%async_computation.3 | async-start | bytes 1032192 | tf_op jit(solution)/shard_map/reduce_scatter | solution.py:122
  47.7 17.1 %collective-permute-start.4 = (bf16[3,640]{1,0:T(4,128)(2,1)S(1)}, bf16[3,640]{1,0:T(4,128)(2,1)S(1)}, u32[]{:S(2)}, u32[]{:S(2)}) collective-permute-start(bf16[3,640]{1,0:T(4,128)(2,1)S(1)} %fusion.89), channel_id=1, source_target_pairs={{0,8},{8,16},{16,24},{24,32},{32,40},{40,48},{48,56},{56,64},{64,7... | collective-permute-start | bytes 11528 | tf_op jit(solution)/shard_map/ppermute | solution.py:15
  51.2 9.0 %collective-permute-start.3 = (s32[3]{0:T(128)S(1)}, s32[3]{0:T(128)S(1)}, u32[]{:S(2)}, u32[]{:S(2)}) collective-permute-start(s32[3]{0:T(128)S(1)} %get-tuple-element.173), channel_id=1, source_target_pairs={{0,8},{8,16},{16,24},{24,32},{32,40},{40,48},{48,56},{56,64},{64,7... | collective-permute-start | bytes 44 | tf_op jit(solution)/shard_map/ppermute | solution.py:15
  54.3 7.8 %collective-permute-start.9 = (s32[3]{0:T(128)S(1)}, s32[3]{0:T(128)S(1)}, u32[]{:S(2)}, u32[]{:S(2)}) collective-permute-start(s32[3]{0:T(128)S(1)} %get-tuple-element.172), channel_id=1, source_target_pairs={{0,8},{8,16},{16,24},{24,32},{32,40},{40,48},{48,56},{56,64},{64,7... | collective-permute-start | bytes 44 | tf_op jit(solution)/shard_map/ppermute | solution.py:15
  66.3 6.9 collective-permute-start
  73.3 6.9 collective-permute-start
  80.3 6.9 collective-permute-start
  87.3 7.8 %collective-permute-start = (bf16[8,64,64]{2,1,0:T(8,128)(2,1)S(1)}, bf16[8,64,64]{2,1,0:T(8,128)(2,1)S(1)}, u32[]{:S(2)}, u32[]{:S(2)}) collective-permute-start(bf16[8,64,64]{2,1,0:T(8,128)(2,1)S(1)} %fusion.132), channel_id=1, source_target_pairs={{0,8},{8,16},{16,24},{24,32},{32,40},{40,48},{48,56},{56,64},{64,7... | collective-permute-start | bytes 196616 | tf_op jit(solution)/shard_map/while/body/eval_jaxpr/ppermute | solution.py:15
  95.2 9.0 %collective-permute-start = (bf16[8,64,64]{2,1,0:T(8,128)(2,1)S(1)}, bf16[8,64,64]{2,1,0:T(8,128)(2,1)S(1)}, u32[]{:S(2)}, u32[]{:S(2)}) collective-permute-start(bf16[8,64,64]{2,1,0:T(8,128)(2,1)S(1)} %fusion.132), channel_id=1, source_target_pairs={{0,8},{8,16},{16,24},{24,32},{32,40},{40,48},{48,56},{56,64},{64,7... | collective-permute-start | bytes 196616 | tf_op jit(solution)/shard_map/while/body/eval_jaxpr/ppermute | solution.py:15
  104.4 9.0 %collective-permute-start = (bf16[8,64,64]{2,1,0:T(8,128)(2,1)S(1)}, bf16[8,64,64]{2,1,0:T(8,128)(2,1)S(1)}, u32[]{:S(2)}, u32[]{:S(2)}) collective-permute-start(bf16[8,64,64]{2,1,0:T(8,128)(2,1)S(1)} %fusion.132), channel_id=1, source_target_pairs={{0,8},{8,16},{16,24},{24,32},{32,40},{40,48},{48,56},{56,64},{64,7... | collective-permute-start | bytes 196616 | tf_op jit(solution)/shard_map/while/body/eval_jaxpr/ppermute | solution.py:15
  113.5 9.0 %collective-permute-start = (bf16[8,64,64]{2,1,0:T(8,128)(2,1)S(1)}, bf16[8,64,64]{2,1,0:T(8,128)(2,1)S(1)}, u32[]{:S(2)}, u32[]{:S(2)}) collective-permute-start(bf16[8,64,64]{2,1,0:T(8,128)(2,1)S(1)} %fusion.132), channel_id=1, source_target_pairs={{0,8},{8,16},{16,24},{24,32},{32,40},{40,48},{48,56},{56,64},{64,7... | collective-permute-start | bytes 196616 | tf_op jit(solution)/shard_map/while/body/eval_jaxpr/ppermute | solution.py:15
  122.6 9.2 %collective-permute-start = (bf16[8,64,64]{2,1,0:T(8,128)(2,1)S(1)}, bf16[8,64,64]{2,1,0:T(8,128)(2,1)S(1)}, u32[]{:S(2)}, u32[]{:S(2)}) collective-permute-start(bf16[8,64,64]{2,1,0:T(8,128)(2,1)S(1)} %fusion.132), channel_id=1, source_target_pairs={{0,8},{8,16},{16,24},{24,32},{32,40},{40,48},{48,56},{56,64},{64,7... | collective-permute-start | bytes 196616 | tf_op jit(solution)/shard_map/while/body/eval_jaxpr/ppermute | solution.py:15
  132.0 10.6 %collective-permute-start = (bf16[8,64,64]{2,1,0:T(8,128)(2,1)S(1)}, bf16[8,64,64]{2,1,0:T(8,128)(2,1)S(1)}, u32[]{:S(2)}, u32[]{:S(2)}) collective-permute-start(bf16[8,64,64]{2,1,0:T(8,128)(2,1)S(1)} %fusion.132), channel_id=1, source_target_pairs={{0,8},{8,16},{16,24},{24,32},{32,40},{40,48},{48,56},{56,64},{64,7... | collective-permute-start | bytes 196616 | tf_op jit(solution)/shard_map/while/body/eval_jaxpr/ppermute | solution.py:15
  142.7 9.1 %collective-permute-start = (bf16[8,64,64]{2,1,0:T(8,128)(2,1)S(1)}, bf16[8,64,64]{2,1,0:T(8,128)(2,1)S(1)}, u32[]{:S(2)}, u32[]{:S(2)}) collective-permute-start(bf16[8,64,64]{2,1,0:T(8,128)(2,1)S(1)} %fusion.132), channel_id=1, source_target_pairs={{0,8},{8,16},{16,24},{24,32},{32,40},{40,48},{48,56},{56,64},{64,7... | collective-permute-start | bytes 196616 | tf_op jit(solution)/shard_map/while/body/eval_jaxpr/ppermute | solution.py:15
  152.0 8.5 %collective-permute-start = (bf16[8,64,64]{2,1,0:T(8,128)(2,1)S(1)}, bf16[8,64,64]{2,1,0:T(8,128)(2,1)S(1)}, u32[]{:S(2)}, u32[]{:S(2)}) collective-permute-start(bf16[8,64,64]{2,1,0:T(8,128)(2,1)S(1)} %fusion.132), channel_id=1, source_target_pairs={{0,8},{8,16},{16,24},{24,32},{32,40},{40,48},{48,56},{56,64},{64,7... | collective-permute-start | bytes 196616 | tf_op jit(solution)/shard_map/while/body/eval_jaxpr/ppermute | solution.py:15
  160.7 9.0 %collective-permute-start = (bf16[8,64,64]{2,1,0:T(8,128)(2,1)S(1)}, bf16[8,64,64]{2,1,0:T(8,128)(2,1)S(1)}, u32[]{:S(2)}, u32[]{:S(2)}) collective-permute-start(bf16[8,64,64]{2,1,0:T(8,128)(2,1)S(1)} %fusion.132), channel_id=1, source_target_pairs={{0,8},{8,16},{16,24},{24,32},{32,40},{40,48},{48,56},{56,64},{64,7... | collective-permute-start | bytes 196616 | tf_op jit(solution)/shard_map/while/body/eval_jaxpr/ppermute | solution.py:15
  169.8 9.0 %collective-permute-start = (bf16[8,64,64]{2,1,0:T(8,128)(2,1)S(1)}, bf16[8,64,64]{2,1,0:T(8,128)(2,1)S(1)}, u32[]{:S(2)}, u32[]{:S(2)}) collective-permute-start(bf16[8,64,64]{2,1,0:T(8,128)(2,1)S(1)} %fusion.132), channel_id=1, source_target_pairs={{0,8},{8,16},{16,24},{24,32},{32,40},{40,48},{48,56},{56,64},{64,7... | collective-permute-start | bytes 196616 | tf_op jit(solution)/shard_map/while/body/eval_jaxpr/ppermute | solution.py:15
  178.9 9.0 %collective-permute-start = (bf16[8,64,64]{2,1,0:T(8,128)(2,1)S(1)}, bf16[8,64,64]{2,1,0:T(8,128)(2,1)S(1)}, u32[]{:S(2)}, u32[]{:S(2)}) collective-permute-start(bf16[8,64,64]{2,1,0:T(8,128)(2,1)S(1)} %fusion.132), channel_id=1, source_target_pairs={{0,8},{8,16},{16,24},{24,32},{32,40},{40,48},{48,56},{56,64},{64,7... | collective-permute-start | bytes 196616 | tf_op jit(solution)/shard_map/while/body/eval_jaxpr/ppermute | solution.py:15
  188.1 9.0 %collective-permute-start = (bf16[8,64,64]{2,1,0:T(8,128)(2,1)S(1)}, bf16[8,64,64]{2,1,0:T(8,128)(2,1)S(1)}, u32[]{:S(2)}, u32[]{:S(2)}) collective-permute-start(bf16[8,64,64]{2,1,0:T(8,128)(2,1)S(1)} %fusion.132), channel_id=1, source_target_pairs={{0,8},{8,16},{16,24},{24,32},{32,40},{40,48},{48,56},{56,64},{64,7... | collective-permute-start | bytes 196616 | tf_op jit(solution)/shard_map/while/body/eval_jaxpr/ppermute | solution.py:15
  218.5 287.9 %reduce-scatter.6.cloned.1.call-start = ((), (), s32[]{:S(2)}) async-start(), calls=%async_computation.4 | async-start | bytes 1032192 | tf_op jit(solution)/shard_map/reduce_scatter | solution.py:122
  218.6 7.7 %collective-permute-start.6 = (s32[3]{0:T(128)S(1)}, s32[3]{0:T(128)S(1)}, u32[]{:S(2)}, u32[]{:S(2)}) collective-permute-start(s32[3]{0:T(128)S(1)} %slice.224), channel_id=1, source_target_pairs={{0,8},{8,16},{16,24},{24,32},{32,40},{40,48},{48,56},{56,64},{64,7... | collective-permute-start | bytes 44 | tf_op jit(solution)/shard_map/ppermute | solution.py:15
  321.5 7.6 %collective-permute-start.1 = (bf16[8,64,64]{2,1,0:T(8,128)(2,1)S(1)}, bf16[8,64,64]{2,1,0:T(8,128)(2,1)S(1)}, u32[]{:S(2)}, u32[]{:S(2)}) collective-permute-start(bf16[8,64,64]{2,1,0:T(8,128)(2,1)S(1)} %fusion.133), channel_id=1, source_target_pairs={{0,8},{8,16},{16,24},{24,32},{32,40},{40,48},{48,56},{56,64},{64,7... | collective-permute-start | bytes 196616 | tf_op jit(solution)/shard_map/while/body/eval_jaxpr/ppermute | solution.py:15
  329.3 8.8 %collective-permute-start.1 = (bf16[8,64,64]{2,1,0:T(8,128)(2,1)S(1)}, bf16[8,64,64]{2,1,0:T(8,128)(2,1)S(1)}, u32[]{:S(2)}, u32[]{:S(2)}) collective-permute-start(bf16[8,64,64]{2,1,0:T(8,128)(2,1)S(1)} %fusion.133), channel_id=1, source_target_pairs={{0,8},{8,16},{16,24},{24,32},{32,40},{40,48},{48,56},{56,64},{64,7... | collective-permute-start | bytes 196616 | tf_op jit(solution)/shard_map/while/body/eval_jaxpr/ppermute | solution.py:15
  338.2 9.0 %collective-permute-start.1 = (bf16[8,64,64]{2,1,0:T(8,128)(2,1)S(1)}, bf16[8,64,64]{2,1,0:T(8,128)(2,1)S(1)}, u32[]{:S(2)}, u32[]{:S(2)}) collective-permute-start(bf16[8,64,64]{2,1,0:T(8,128)(2,1)S(1)} %fusion.133), channel_id=1, source_target_pairs={{0,8},{8,16},{16,24},{24,32},{32,40},{40,48},{48,56},{56,64},{64,7... | collective-permute-start | bytes 196616 | tf_op jit(solution)/shard_map/while/body/eval_jaxpr/ppermute | solution.py:15
  347.4 9.0 %collective-permute-start.1 = (bf16[8,64,64]{2,1,0:T(8,128)(2,1)S(1)}, bf16[8,64,64]{2,1,0:T(8,128)(2,1)S(1)}, u32[]{:S(2)}, u32[]{:S(2)}) collective-permute-start(bf16[8,64,64]{2,1,0:T(8,128)(2,1)S(1)} %fusion.133), channel_id=1, source_target_pairs={{0,8},{8,16},{16,24},{24,32},{32,40},{40,48},{48,56},{56,64},{64,7... | collective-permute-start | bytes 196616 | tf_op jit(solution)/shard_map/while/body/eval_jaxpr/ppermute | solution.py:15
  356.5 9.0 %collective-permute-start.1 = (bf16[8,64,64]{2,1,0:T(8,128)(2,1)S(1)}, bf16[8,64,64]{2,1,0:T(8,128)(2,1)S(1)}, u32[]{:S(2)}, u32[]{:S(2)}) collective-permute-start(bf16[8,64,64]{2,1,0:T(8,128)(2,1)S(1)} %fusion.133), channel_id=1, source_target_pairs={{0,8},{8,16},{16,24},{24,32},{32,40},{40,48},{48,56},{56,64},{64,7... | collective-permute-start | bytes 196616 | tf_op jit(solution)/shard_map/while/body/eval_jaxpr/ppermute | solution.py:15
  365.6 9.2 %collective-permute-start.1 = (bf16[8,64,64]{2,1,0:T(8,128)(2,1)S(1)}, bf16[8,64,64]{2,1,0:T(8,128)(2,1)S(1)}, u32[]{:S(2)}, u32[]{:S(2)}) collective-permute-start(bf16[8,64,64]{2,1,0:T(8,128)(2,1)S(1)} %fusion.133), channel_id=1, source_target_pairs={{0,8},{8,16},{16,24},{24,32},{32,40},{40,48},{48,56},{56,64},{64,7... | collective-permute-start | bytes 196616 | tf_op jit(solution)/shard_map/while/body/eval_jaxpr/ppermute | solution.py:15
  375.0 10.6 %collective-permute-start.1 = (bf16[8,64,64]{2,1,0:T(8,128)(2,1)S(1)}, bf16[8,64,64]{2,1,0:T(8,128)(2,1)S(1)}, u32[]{:S(2)}, u32[]{:S(2)}) collective-permute-start(bf16[8,64,64]{2,1,0:T(8,128)(2,1)S(1)} %fusion.133), channel_id=1, source_target_pairs={{0,8},{8,16},{16,24},{24,32},{32,40},{40,48},{48,56},{56,64},{64,7... | collective-permute-start | bytes 196616 | tf_op jit(solution)/shard_map/while/body/eval_jaxpr/ppermute | solution.py:15
  385.7 9.1 %collective-permute-start.1 = (bf16[8,64,64]{2,1,0:T(8,128)(2,1)S(1)}, bf16[8,64,64]{2,1,0:T(8,128)(2,1)S(1)}, u32[]{:S(2)}, u32[]{:S(2)}) collective-permute-start(bf16[8,64,64]{2,1,0:T(8,128)(2,1)S(1)} %fusion.133), channel_id=1, source_target_pairs={{0,8},{8,16},{16,24},{24,32},{32,40},{40,48},{48,56},{56,64},{64,7... | collective-permute-start | bytes 196616 | tf_op jit(solution)/shard_map/while/body/eval_jaxpr/ppermute | solution.py:15
  395.0 8.5 %collective-permute-start.1 = (bf16[8,64,64]{2,1,0:T(8,128)(2,1)S(1)}, bf16[8,64,64]{2,1,0:T(8,128)(2,1)S(1)}, u32[]{:S(2)}, u32[]{:S(2)}) collective-permute-start(bf16[8,64,64]{2,1,0:T(8,128)(2,1)S(1)} %fusion.133), channel_id=1, source_target_pairs={{0,8},{8,16},{16,24},{24,32},{32,40},{40,48},{48,56},{56,64},{64,7... | collective-permute-start | bytes 196616 | tf_op jit(solution)/shard_map/while/body/eval_jaxpr/ppermute | solution.py:15
  403.7 9.0 %collective-permute-start.1 = (bf16[8,64,64]{2,1,0:T(8,128)(2,1)S(1)}, bf16[8,64,64]{2,1,0:T(8,128)(2,1)S(1)}, u32[]{:S(2)}, u32[]{:S(2)}) collective-permute-start(bf16[8,64,64]{2,1,0:T(8,128)(2,1)S(1)} %fusion.133), channel_id=1, source_target_pairs={{0,8},{8,16},{16,24},{24,32},{32,40},{40,48},{48,56},{56,64},{64,7... | collective-permute-start | bytes 196616 | tf_op jit(solution)/shard_map/while/body/eval_jaxpr/ppermute | solution.py:15
  412.9 9.0 %collective-permute-start.1 = (bf16[8,64,64]{2,1,0:T(8,128)(2,1)S(1)}, bf16[8,64,64]{2,1,0:T(8,128)(2,1)S(1)}, u32[]{:S(2)}, u32[]{:S(2)}) collective-permute-start(bf16[8,64,64]{2,1,0:T(8,128)(2,1)S(1)} %fusion.133), channel_id=1, source_target_pairs={{0,8},{8,16},{16,24},{24,32},{32,40},{40,48},{48,56},{56,64},{64,7... | collective-permute-start | bytes 196616 | tf_op jit(solution)/shard_map/while/body/eval_jaxpr/ppermute | solution.py:15
  422.0 9.0 %collective-permute-start.1 = (bf16[8,64,64]{2,1,0:T(8,128)(2,1)S(1)}, bf16[8,64,64]{2,1,0:T(8,128)(2,1)S(1)}, u32[]{:S(2)}, u32[]{:S(2)}) collective-permute-start(bf16[8,64,64]{2,1,0:T(8,128)(2,1)S(1)} %fusion.133), channel_id=1, source_target_pairs={{0,8},{8,16},{16,24},{24,32},{32,40},{40,48},{48,56},{56,64},{64,7... | collective-permute-start | bytes 196616 | tf_op jit(solution)/shard_map/while/body/eval_jaxpr/ppermute | solution.py:15
  431.1 9.0 %collective-permute-start.1 = (bf16[8,64,64]{2,1,0:T(8,128)(2,1)S(1)}, bf16[8,64,64]{2,1,0:T(8,128)(2,1)S(1)}, u32[]{:S(2)}, u32[]{:S(2)}) collective-permute-start(bf16[8,64,64]{2,1,0:T(8,128)(2,1)S(1)} %fusion.133), channel_id=1, source_target_pairs={{0,8},{8,16},{16,24},{24,32},{32,40},{40,48},{48,56},{56,64},{64,7... | collective-permute-start | bytes 196616 | tf_op jit(solution)/shard_map/while/body/eval_jaxpr/ppermute | solution.py:15
  461.3 288.9 %reduce-scatter.8.cloned.1.call-start = ((), (), s32[]{:S(2)}) async-start(), calls=%async_computation.5 | async-start | bytes 1032192 | tf_op jit(solution)/shard_map/reduce_scatter | solution.py:122
  565.2 7.2 collective-permute-start.2
  572.6 9.0 %collective-permute-start.2 = (bf16[8,64,64]{2,1,0:T(8,128)(2,1)S(1)}, bf16[8,64,64]{2,1,0:T(8,128)(2,1)S(1)}, u32[]{:S(2)}, u32[]{:S(2)}) collective-permute-start(bf16[8,64,64]{2,1,0:T(8,128)(2,1)S(1)} %fusion.134), channel_id=1, source_target_pairs={{0,8},{8,16},{16,24},{24,32},{32,40},{40,48},{48,56},{56,64},{64,7... | collective-permute-start | bytes 196616 | tf_op jit(solution)/shard_map/while/body/eval_jaxpr/ppermute | solution.py:15
  581.7 9.0 %collective-permute-start.2 = (bf16[8,64,64]{2,1,0:T(8,128)(2,1)S(1)}, bf16[8,64,64]{2,1,0:T(8,128)(2,1)S(1)}, u32[]{:S(2)}, u32[]{:S(2)}) collective-permute-start(bf16[8,64,64]{2,1,0:T(8,128)(2,1)S(1)} %fusion.134), channel_id=1, source_target_pairs={{0,8},{8,16},{16,24},{24,32},{32,40},{40,48},{48,56},{56,64},{64,7... | collective-permute-start | bytes 196616 | tf_op jit(solution)/shard_map/while/body/eval_jaxpr/ppermute | solution.py:15
  590.9 9.0 %collective-permute-start.2 = (bf16[8,64,64]{2,1,0:T(8,128)(2,1)S(1)}, bf16[8,64,64]{2,1,0:T(8,128)(2,1)S(1)}, u32[]{:S(2)}, u32[]{:S(2)}) collective-permute-start(bf16[8,64,64]{2,1,0:T(8,128)(2,1)S(1)} %fusion.134), channel_id=1, source_target_pairs={{0,8},{8,16},{16,24},{24,32},{32,40},{40,48},{48,56},{56,64},{64,7... | collective-permute-start | bytes 196616 | tf_op jit(solution)/shard_map/while/body/eval_jaxpr/ppermute | solution.py:15
  600.0 9.0 %collective-permute-start.2 = (bf16[8,64,64]{2,1,0:T(8,128)(2,1)S(1)}, bf16[8,64,64]{2,1,0:T(8,128)(2,1)S(1)}, u32[]{:S(2)}, u32[]{:S(2)}) collective-permute-start(bf16[8,64,64]{2,1,0:T(8,128)(2,1)S(1)} %fusion.134), channel_id=1, source_target_pairs={{0,8},{8,16},{16,24},{24,32},{32,40},{40,48},{48,56},{56,64},{64,7... | collective-permute-start | bytes 196616 | tf_op jit(solution)/shard_map/while/body/eval_jaxpr/ppermute | solution.py:15
  609.1 9.4 %collective-permute-start.2 = (bf16[8,64,64]{2,1,0:T(8,128)(2,1)S(1)}, bf16[8,64,64]{2,1,0:T(8,128)(2,1)S(1)}, u32[]{:S(2)}, u32[]{:S(2)}) collective-permute-start(bf16[8,64,64]{2,1,0:T(8,128)(2,1)S(1)} %fusion.134), channel_id=1, source_target_pairs={{0,8},{8,16},{16,24},{24,32},{32,40},{40,48},{48,56},{56,64},{64,7... | collective-permute-start | bytes 196616 | tf_op jit(solution)/shard_map/while/body/eval_jaxpr/ppermute | solution.py:15
  618.6 10.4 %collective-permute-start.2 = (bf16[8,64,64]{2,1,0:T(8,128)(2,1)S(1)}, bf16[8,64,64]{2,1,0:T(8,128)(2,1)S(1)}, u32[]{:S(2)}, u32[]{:S(2)}) collective-permute-start(bf16[8,64,64]{2,1,0:T(8,128)(2,1)S(1)} %fusion.134), channel_id=1, source_target_pairs={{0,8},{8,16},{16,24},{24,32},{32,40},{40,48},{48,56},{56,64},{64,7... | collective-permute-start | bytes 196616 | tf_op jit(solution)/shard_map/while/body/eval_jaxpr/ppermute | solution.py:15
  629.2 9.0 %collective-permute-start.2 = (bf16[8,64,64]{2,1,0:T(8,128)(2,1)S(1)}, bf16[8,64,64]{2,1,0:T(8,128)(2,1)S(1)}, u32[]{:S(2)}, u32[]{:S(2)}) collective-permute-start(bf16[8,64,64]{2,1,0:T(8,128)(2,1)S(1)} %fusion.134), channel_id=1, source_target_pairs={{0,8},{8,16},{16,24},{24,32},{32,40},{40,48},{48,56},{56,64},{64,7... | collective-permute-start | bytes 196616 | tf_op jit(solution)/shard_map/while/body/eval_jaxpr/ppermute | solution.py:15
  638.3 8.7 %collective-permute-start.2 = (bf16[8,64,64]{2,1,0:T(8,128)(2,1)S(1)}, bf16[8,64,64]{2,1,0:T(8,128)(2,1)S(1)}, u32[]{:S(2)}, u32[]{:S(2)}) collective-permute-start(bf16[8,64,64]{2,1,0:T(8,128)(2,1)S(1)} %fusion.134), channel_id=1, source_target_pairs={{0,8},{8,16},{16,24},{24,32},{32,40},{40,48},{48,56},{56,64},{64,7... | collective-permute-start | bytes 196616 | tf_op jit(solution)/shard_map/while/body/eval_jaxpr/ppermute | solution.py:15
  647.2 9.0 %collective-permute-start.2 = (bf16[8,64,64]{2,1,0:T(8,128)(2,1)S(1)}, bf16[8,64,64]{2,1,0:T(8,128)(2,1)S(1)}, u32[]{:S(2)}, u32[]{:S(2)}) collective-permute-start(bf16[8,64,64]{2,1,0:T(8,128)(2,1)S(1)} %fusion.134), channel_id=1, source_target_pairs={{0,8},{8,16},{16,24},{24,32},{32,40},{40,48},{48,56},{56,64},{64,7... | collective-permute-start | bytes 196616 | tf_op jit(solution)/shard_map/while/body/eval_jaxpr/ppermute | solution.py:15
  656.3 9.0 %collective-permute-start.2 = (bf16[8,64,64]{2,1,0:T(8,128)(2,1)S(1)}, bf16[8,64,64]{2,1,0:T(8,128)(2,1)S(1)}, u32[]{:S(2)}, u32[]{:S(2)}) collective-permute-start(bf16[8,64,64]{2,1,0:T(8,128)(2,1)S(1)} %fusion.134), channel_id=1, source_target_pairs={{0,8},{8,16},{16,24},{24,32},{32,40},{40,48},{48,56},{56,64},{64,7... | collective-permute-start | bytes 196616 | tf_op jit(solution)/shard_map/while/body/eval_jaxpr/ppermute | solution.py:15
  665.4 9.0 %collective-permute-start.2 = (bf16[8,64,64]{2,1,0:T(8,128)(2,1)S(1)}, bf16[8,64,64]{2,1,0:T(8,128)(2,1)S(1)}, u32[]{:S(2)}, u32[]{:S(2)}) collective-permute-start(bf16[8,64,64]{2,1,0:T(8,128)(2,1)S(1)} %fusion.134), channel_id=1, source_target_pairs={{0,8},{8,16},{16,24},{24,32},{32,40},{40,48},{48,56},{56,64},{64,7... | collective-permute-start | bytes 196616 | tf_op jit(solution)/shard_map/while/body/eval_jaxpr/ppermute | solution.py:15
  674.6 9.0 %collective-permute-start.2 = (bf16[8,64,64]{2,1,0:T(8,128)(2,1)S(1)}, bf16[8,64,64]{2,1,0:T(8,128)(2,1)S(1)}, u32[]{:S(2)}, u32[]{:S(2)}) collective-permute-start(bf16[8,64,64]{2,1,0:T(8,128)(2,1)S(1)} %fusion.134), channel_id=1, source_target_pairs={{0,8},{8,16},{16,24},{24,32},{32,40},{40,48},{48,56},{56,64},{64,7... | collective-permute-start | bytes 196616 | tf_op jit(solution)/shard_map/while/body/eval_jaxpr/ppermute | solution.py:15
  (21 other events, 454.1 us)
Sparse Core Ops, SparseCore 0:
  218.6 43.9 reduce-scatter.3
  461.4 44.9 reduce-scatter.5
  705.0 45.1 reduce-scatter.7
where the time goes:
time: 760 us; the launch traced here: 758 us
  starting transfers between devices  291 us (38%)
  waiting for transfers between devices  254 us (33%)
  blocking collectives  132 us (17%)
  matrix products  34.3 us (5%)
  other arithmetic  18.3 us (2%)
  between operations  17.5 us (2%)
  local copies, waits for them, and re-layouts  10.9 us (1%)
    ppermute x53, starting transfers between devices, shifted(): return lax.ppermute(block, axis, route)  291 us
    ppermute x53, waiting for transfers between devices, shifted(): return lax.ppermute(block, axis, route)  129 us
    reduce_scatter x3, waiting for transfers between devices, mixer_layer(): lax.psum_scatter(update.astype(jnp.bfloat16), 'mp', scatter_dimension=1,...  125 us
    all_gather x3, blocking collectives, mixer_layer(): whole = lax.all_gather(hidden_rows, 'mp', axis=1, tiled=True)  83.3 us
    psum x3, blocking collectives, mixer_layer(): squares = lax.psum(jnp.sum(gated * gated, axis=-1), 'mp')  48.2 us
  transfers between devices with their start and end apart: 56, of which 51 were waited for; matrix products, arithmetic and copies ran while one was open for 1% of the time, Pallas kernels for 0%

commit v1 on v0

--- a/solution.py
+++ b/solution.py
@@ -73,7 +73,9 @@
     inner_gain,
     out_weight,
 ):
-    whole = lax.all_gather(hidden_rows, "mp", axis=1, tiled=True)
+    kept_arr = jnp.stack([hidden_rows for _ in range(lax.axis_size("mp"))])
+    x_new = lax.all_to_all(kept_arr, "mp", split_axis=0, concat_axis=0)
+    whole = jnp.concatenate(x_new, axis=1)
     normed = norm_rows(whole, norm_gain)
     width_loc = in_weight.shape[-1]
     both = jnp.dot(

time: 760 us -> 753 us (level)
  blocking collectives: 132 us -> 46.1 us
  waiting for transfers between devices: 254 us -> 315 us
  starting transfers between devices: 291 us -> 303 us
    all_gather x3 -> x0, blocking collectives: 83.3 us -> none  [mixer_layer(): whole = lax.all_gather(hidden_rows, 'mp', axis=1, tiled=True)]
    all_to_all x0 -> x3, waiting for transfers between devices: none -> 47.1 us  [mixer_layer(): x_new = lax.all_to_all(kept_arr, 'mp', split_axis=0, concat_axis=0)]
    all_to_all x0 -> x3, starting transfers between devices: none -> 17.2 us  [mixer_layer(): x_new = lax.all_to_all(kept_arr, 'mp', split_axis=0, concat_axis=0)]
  transfers between devices with their start and end apart: 56 -> 59, of which waited for: 51 -> 57; matrix products, arithmetic and copies ran while one was open for 1% -> 2% of each run, Pallas kernels for 0% -> 0%
where the time goes in v1:
time: 753 us; the launch traced here: 751 us
  waiting for transfers between devices  315 us (42%)
  starting transfers between devices  303 us (40%)
  blocking collectives  46.1 us (6%)
  matrix products  32 us (4%)
  other arithmetic  20 us (3%)
  between operations  17.6 us (2%)
  local copies, waits for them, and re-layouts  16.3 us (2%)
    ppermute x53, starting transfers between devices, shifted(): return lax.ppermute(block, axis, route)  285 us
    ppermute x53, waiting for transfers between devices, shifted(): return lax.ppermute(block, axis, route)  136 us
    reduce_scatter x3, waiting for transfers between devices, mixer_layer(): lax.psum_scatter(update.astype(jnp.bfloat16), 'mp', scatter_dimension=1,...  132 us
    all_to_all x3, waiting for transfers between devices, mixer_layer(): x_new = lax.all_to_all(kept_arr, 'mp', split_axis=0, concat_axis=0)  47.1 us
    psum x3, blocking collectives, mixer_layer(): squares = lax.psum(jnp.sum(gated * gated, axis=-1), 'mp')  46.1 us
    all_to_all x3, starting transfers between devices, mixer_layer(): x_new = lax.all_to_all(kept_arr, 'mp', split_axis=0, concat_axis=0)  17.2 us
  transfers between devices with their start and end apart: 59, of which 57 were waited for; matrix products, arithmetic and copies ran while one was open for 2% of the time, Pallas kernels for 0%

profile of v1, /device:TPU:2, one launch (start us, length us, event | category | flops | bytes accessed | tf_op | source)
XLA Modules:
  0.0 750.9 jit_solution(9121572691785536222)
XLA Ops:
  8.6 8.5 %all-to-all-start = ((bf16[8,128,448]{1,2,0:T(8,128)(2,1)}), bf16[8,128,448]{1,2,0:T(8,128)(2,1)S(1)}, u32[]{:S(2)}, u32[]{:S(2)}) async-start(bf16[8,128,448]{1,2,0:T(8,128)(2,1)} %stack.12), calls=%async_computation | async-start | bytes 1835008 | tf_op jit(solution)/shard_map/all_to_all | solution.py:77
  23.8 8.4 %copy.83 = bf16[448,8,2,512]{3,1,2,0:T(8,128)(2,1)} copy(bf16[448,8,2,512]{3,2,1,0:T(2,128)(2,1)} %bitcast.180) | data formatting | bytes 14680064
  56.2 132.2 %while.33 = (s32[]{:T(128)}, f32[8,64,64]{2,1,0:T(8,128)S(1)}, f32[8]{0:T(128)S(1)}, f32[8,64,64]{2,1,0:T(8,128)S(1)}, s32[]{:T(128)}, /*index=5*/s32[]{:T(128)}) while((s32[]{:T(128)}, f32[8,64,64]{2,1,0:T(8,128)S(1)}, f32[8]{0:T(128)S(1)}, f32[8,64,64]{2,1,0:T(8,128)S(1)}, s32[]{:T(128)}, /*index=5*/s32[]{:T(128)}) %tuple.86), condition=%wide.region_3.4_spmd.clone, body=%wide.region_2.3_spmd.clone.sunk | while | flops 163843 | bytes 786583 | solution.py:110
  77.4 5.4 collective-permute-start
  85.4 6.5 collective-permute-start
  94.5 6.5 collective-permute-start
  104.3 6.9 collective-permute-start
  114.8 6.6 collective-permute-start
  124.0 6.3 collective-permute-start
  132.9 6.5 collective-permute-start
  142.1 6.5 collective-permute-start
  151.2 6.5 collective-permute-start
  160.3 6.5 collective-permute-start
  169.7 6.8 collective-permute-start
  179.1 6.8 collective-permute-start
  189.1 15.7 %psum.21 = f32[128]{0:T(128)S(1)} all-reduce(f32[128]{0:T(128)S(1)} %multiply_reduce_fusion.2), channel_id=1, replica_groups=mesh['section'=2,'seq'=16,'mp'=8] {'mp'}, use_global_device_ids=true, to_apply=%region_5.6 | all-reduce | flops 128 | bytes 1024 | tf_op jit(solution)/shard_map/psum | solution.py:120
  209.5 43.8 %reduce-scatter.4.cloned.1.call-done = bf16[128,448]{0,1:T(8,128)(2,1)} async-done(((bf16[128,3584]{0,1:T(8,128)(2,1)}), bf16[128,448]{0,1:T(8,128)(2,1)}) %reduce-scatter.4.cloned.1.call-update) | async-done | bytes 114704 | tf_op jit(solution)/shard_map/reduce_scatter | solution.py:124
  270.9 17.4 %all-to-all-done.1 = bf16[8,128,448]{1,2,0:T(8,128)(2,1)S(1)} async-done(((bf16[8,128,448]{1,2,0:T(8,128)(2,1)}), bf16[8,128,448]{1,2,0:T(8,128)(2,1)S(1)}, u32[]{:S(2)}, u32[]{:S(2)}) %all-to-all-start.1) | async-done | bytes 917536 | tf_op jit(solution)/shard_map/all_to_all | solution.py:77
  301.6 132.1 %while.34 = (s32[]{:T(128)}, f32[8,64,64]{2,1,0:T(8,128)S(1)}, f32[8]{0:T(128)S(1)}, f32[8,64,64]{2,1,0:T(8,128)S(1)}, s32[]{:T(128)}, /*index=5*/s32[]{:T(128)}) while((s32[]{:T(128)}, f32[8,64,64]{2,1,0:T(8,128)S(1)}, f32[8]{0:T(128)S(1)}, f32[8,64,64]{2,1,0:T(8,128)S(1)}, s32[]{:T(128)}, /*index=5*/s32[]{:T(128)}) %tuple.89), condition=%wide.region_10.11_spmd.clone, body=%wide.region_9.10_spmd.clone.sunk | while | flops 163843 | bytes 786583 | solution.py:110
  330.7 6.5 collective-permute-start.1
  339.8 6.5 collective-permute-start.1
  349.6 6.8 collective-permute-start.1
  360.0 6.5 collective-permute-start.1
  369.2 6.3 collective-permute-start.1
  378.2 6.5 collective-permute-start.1
  387.3 6.5 collective-permute-start.1
  396.4 6.5 collective-permute-start.1
  405.6 6.5 collective-permute-start.1
  414.9 6.8 collective-permute-start.1
  424.4 6.8 collective-permute-start.1
  434.3 15.2 %psum.22 = f32[128]{0:T(128)S(1)} all-reduce(f32[128]{0:T(128)S(1)} %multiply_reduce_fusion.1), channel_id=1, replica_groups=mesh['section'=2,'seq'=16,'mp'=8] {'mp'}, use_global_device_ids=true, to_apply=%region_12.13 | all-reduce | flops 128 | bytes 1024 | tf_op jit(solution)/shard_map/psum | solution.py:120
  454.2 43.9 %reduce-scatter.6.cloned.1.call-done = bf16[128,448]{0,1:T(8,128)(2,1)} async-done(((bf16[128,3584]{0,1:T(8,128)(2,1)}), bf16[128,448]{0,1:T(8,128)(2,1)}) %reduce-scatter.6.cloned.1.call-update) | async-done | bytes 114704 | tf_op jit(solution)/shard_map/reduce_scatter | solution.py:124
  508.0 25.1 %all-to-all-done.2 = bf16[8,128,448]{1,2,0:T(8,128)(2,1)S(1)} async-done(((bf16[8,128,448]{1,2,0:T(8,128)(2,1)}), bf16[8,128,448]{1,2,0:T(8,128)(2,1)S(1)}, u32[]{:S(2)}, u32[]{:S(2)}) %all-to-all-start.2) | async-done | bytes 917536 | tf_op jit(solution)/shard_map/all_to_all | solution.py:77
  546.3 132.1 %while.35 = (s32[]{:T(128)}, f32[8,64,64]{2,1,0:T(8,128)S(1)}, f32[8]{0:T(128)S(1)}, f32[8,64,64]{2,1,0:T(8,128)S(1)}, s32[]{:T(128)}, /*index=5*/s32[]{:T(128)}) while((s32[]{:T(128)}, f32[8,64,64]{2,1,0:T(8,128)S(1)}, f32[8]{0:T(128)S(1)}, f32[8,64,64]{2,1,0:T(8,128)S(1)}, s32[]{:T(128)}, /*index=5*/s32[]{:T(128)}) %tuple.92), condition=%wide.region_17.18_spmd.clone, body=%wide.region_16.17_spmd.clone.sunk | while | flops 163843 | bytes 786583 | solution.py:110
  567.4 5.4 collective-permute-start.2
  575.4 6.5 collective-permute-start.2
  584.6 6.5 collective-permute-start.2
  594.3 6.8 collective-permute-start.2
  604.8 6.6 collective-permute-start.2
  614.0 6.3 collective-permute-start.2
  622.9 6.5 collective-permute-start.2
  632.1 6.5 collective-permute-start.2
  641.2 6.5 collective-permute-start.2
  650.3 6.5 collective-permute-start.2
  659.7 6.8 collective-permute-start.2
  669.1 6.8 collective-permute-start.2
  679.1 15.2 %psum.23 = f32[128]{0:T(128)S(1)} all-reduce(f32[128]{0:T(128)S(1)} %multiply_reduce_fusion), channel_id=1, replica_groups=mesh['section'=2,'seq'=16,'mp'=8] {'mp'}, use_global_device_ids=true, to_apply=%region_19.20 | all-reduce | flops 128 | bytes 1024 | tf_op jit(solution)/shard_map/psum | solution.py:120
  698.9 43.8 %reduce-scatter.8.cloned.1.call-done = bf16[128,448]{0,1:T(8,128)(2,1)} async-done(((bf16[128,3584]{0,1:T(8,128)(2,1)}), bf16[128,448]{0,1:T(8,128)(2,1)}) %reduce-scatter.8.cloned.1.call-update) | async-done | bytes 114704 | tf_op jit(solution)/shard_map/reduce_scatter | solution.py:124
  (317 shorter events, 267.8 us)
Async XLA Ops:
  8.6 34.4 %all-to-all-start = ((bf16[8,128,448]{1,2,0:T(8,128)(2,1)}), bf16[8,128,448]{1,2,0:T(8,128)(2,1)S(1)}, u32[]{:S(2)}, u32[]{:S(2)}) async-start(bf16[8,128,448]{1,2,0:T(8,128)(2,1)} %stack.12), calls=%async_computation | async-start | bytes 1835008 | tf_op jit(solution)/shard_map/all_to_all | solution.py:77
  17.0 236.2 %reduce-scatter.4.cloned.1.call-start = ((), (), s32[]{:S(2)}) async-start(), calls=%async_computation.6 | async-start | bytes 1032192 | tf_op jit(solution)/shard_map/reduce_scatter | solution.py:124
  17.2 16.6 %collective-permute-start.3 = (s32[3]{0:T(128)S(1)}, s32[3]{0:T(128)S(1)}, u32[]{:S(2)}, u32[]{:S(2)}) collective-permute-start(s32[3]{0:T(128)S(1)} %get-tuple-element.173), channel_id=1, source_target_pairs={{0,8},{8,16},{16,24},{24,32},{32,40},{40,48},{48,56},{56,64},{64,7... | collective-permute-start | bytes 44 | tf_op jit(solution)/shard_map/ppermute | solution.py:15
  20.6 15.2 %collective-permute-start.9 = (s32[3]{0:T(128)S(1)}, s32[3]{0:T(128)S(1)}, u32[]{:S(2)}, u32[]{:S(2)}) collective-permute-start(s32[3]{0:T(128)S(1)} %get-tuple-element.172), channel_id=1, source_target_pairs={{0,8},{8,16},{16,24},{24,32},{32,40},{40,48},{48,56},{56,64},{64,7... | collective-permute-start | bytes 44 | tf_op jit(solution)/shard_map/ppermute | solution.py:15
  56.3 6.9 collective-permute-start
  70.3 6.9 collective-permute-start
  77.4 7.9 %collective-permute-start = (bf16[8,64,64]{2,1,0:T(8,128)(2,1)S(1)}, bf16[8,64,64]{2,1,0:T(8,128)(2,1)S(1)}, u32[]{:S(2)}, u32[]{:S(2)}) collective-permute-start(bf16[8,64,64]{2,1,0:T(8,128)(2,1)S(1)} %fusion.131), channel_id=1, source_target_pairs={{0,8},{8,16},{16,24},{24,32},{32,40},{40,48},{48,56},{56,64},{64,7... | collective-permute-start | bytes 196616 | tf_op jit(solution)/shard_map/while/body/eval_jaxpr/ppermute | solution.py:15
  85.4 9.0 %collective-permute-start = (bf16[8,64,64]{2,1,0:T(8,128)(2,1)S(1)}, bf16[8,64,64]{2,1,0:T(8,128)(2,1)S(1)}, u32[]{:S(2)}, u32[]{:S(2)}) collective-permute-start(bf16[8,64,64]{2,1,0:T(8,128)(2,1)S(1)} %fusion.131), channel_id=1, source_target_pairs={{0,8},{8,16},{16,24},{24,32},{32,40},{40,48},{48,56},{56,64},{64,7... | collective-permute-start | bytes 196616 | tf_op jit(solution)/shard_map/while/body/eval_jaxpr/ppermute | solution.py:15
  94.5 9.6 %collective-permute-start = (bf16[8,64,64]{2,1,0:T(8,128)(2,1)S(1)}, bf16[8,64,64]{2,1,0:T(8,128)(2,1)S(1)}, u32[]{:S(2)}, u32[]{:S(2)}) collective-permute-start(bf16[8,64,64]{2,1,0:T(8,128)(2,1)S(1)} %fusion.131), channel_id=1, source_target_pairs={{0,8},{8,16},{16,24},{24,32},{32,40},{40,48},{48,56},{56,64},{64,7... | collective-permute-start | bytes 196616 | tf_op jit(solution)/shard_map/while/body/eval_jaxpr/ppermute | solution.py:15
  104.3 10.3 %collective-permute-start = (bf16[8,64,64]{2,1,0:T(8,128)(2,1)S(1)}, bf16[8,64,64]{2,1,0:T(8,128)(2,1)S(1)}, u32[]{:S(2)}, u32[]{:S(2)}) collective-permute-start(bf16[8,64,64]{2,1,0:T(8,128)(2,1)S(1)} %fusion.131), channel_id=1, source_target_pairs={{0,8},{8,16},{16,24},{24,32},{32,40},{40,48},{48,56},{56,64},{64,7... | collective-permute-start | bytes 196616 | tf_op jit(solution)/shard_map/while/body/eval_jaxpr/ppermute | solution.py:15
  114.8 9.1 %collective-permute-start = (bf16[8,64,64]{2,1,0:T(8,128)(2,1)S(1)}, bf16[8,64,64]{2,1,0:T(8,128)(2,1)S(1)}, u32[]{:S(2)}, u32[]{:S(2)}) collective-permute-start(bf16[8,64,64]{2,1,0:T(8,128)(2,1)S(1)} %fusion.131), channel_id=1, source_target_pairs={{0,8},{8,16},{16,24},{24,32},{32,40},{40,48},{48,56},{56,64},{64,7... | collective-permute-start | bytes 196616 | tf_op jit(solution)/shard_map/while/body/eval_jaxpr/ppermute | solution.py:15
  124.0 8.8 %collective-permute-start = (bf16[8,64,64]{2,1,0:T(8,128)(2,1)S(1)}, bf16[8,64,64]{2,1,0:T(8,128)(2,1)S(1)}, u32[]{:S(2)}, u32[]{:S(2)}) collective-permute-start(bf16[8,64,64]{2,1,0:T(8,128)(2,1)S(1)} %fusion.131), channel_id=1, source_target_pairs={{0,8},{8,16},{16,24},{24,32},{32,40},{40,48},{48,56},{56,64},{64,7... | collective-permute-start | bytes 196616 | tf_op jit(solution)/shard_map/while/body/eval_jaxpr/ppermute | solution.py:15
  132.9 9.0 %collective-permute-start = (bf16[8,64,64]{2,1,0:T(8,128)(2,1)S(1)}, bf16[8,64,64]{2,1,0:T(8,128)(2,1)S(1)}, u32[]{:S(2)}, u32[]{:S(2)}) collective-permute-start(bf16[8,64,64]{2,1,0:T(8,128)(2,1)S(1)} %fusion.131), channel_id=1, source_target_pairs={{0,8},{8,16},{16,24},{24,32},{32,40},{40,48},{48,56},{56,64},{64,7... | collective-permute-start | bytes 196616 | tf_op jit(solution)/shard_map/while/body/eval_jaxpr/ppermute | solution.py:15
  142.1 9.0 %collective-permute-start = (bf16[8,64,64]{2,1,0:T(8,128)(2,1)S(1)}, bf16[8,64,64]{2,1,0:T(8,128)(2,1)S(1)}, u32[]{:S(2)}, u32[]{:S(2)}) collective-permute-start(bf16[8,64,64]{2,1,0:T(8,128)(2,1)S(1)} %fusion.131), channel_id=1, source_target_pairs={{0,8},{8,16},{16,24},{24,32},{32,40},{40,48},{48,56},{56,64},{64,7... | collective-permute-start | bytes 196616 | tf_op jit(solution)/shard_map/while/body/eval_jaxpr/ppermute | solution.py:15
  151.2 9.0 %collective-permute-start = (bf16[8,64,64]{2,1,0:T(8,128)(2,1)S(1)}, bf16[8,64,64]{2,1,0:T(8,128)(2,1)S(1)}, u32[]{:S(2)}, u32[]{:S(2)}) collective-permute-start(bf16[8,64,64]{2,1,0:T(8,128)(2,1)S(1)} %fusion.131), channel_id=1, source_target_pairs={{0,8},{8,16},{16,24},{24,32},{32,40},{40,48},{48,56},{56,64},{64,7... | collective-permute-start | bytes 196616 | tf_op jit(solution)/shard_map/while/body/eval_jaxpr/ppermute | solution.py:15
  160.3 9.2 %collective-permute-start = (bf16[8,64,64]{2,1,0:T(8,128)(2,1)S(1)}, bf16[8,64,64]{2,1,0:T(8,128)(2,1)S(1)}, u32[]{:S(2)}, u32[]{:S(2)}) collective-permute-start(bf16[8,64,64]{2,1,0:T(8,128)(2,1)S(1)} %fusion.131), channel_id=1, source_target_pairs={{0,8},{8,16},{16,24},{24,32},{32,40},{40,48},{48,56},{56,64},{64,7... | collective-permute-start | bytes 196616 | tf_op jit(solution)/shard_map/while/body/eval_jaxpr/ppermute | solution.py:15
  169.7 9.3 %collective-permute-start = (bf16[8,64,64]{2,1,0:T(8,128)(2,1)S(1)}, bf16[8,64,64]{2,1,0:T(8,128)(2,1)S(1)}, u32[]{:S(2)}, u32[]{:S(2)}) collective-permute-start(bf16[8,64,64]{2,1,0:T(8,128)(2,1)S(1)} %fusion.131), channel_id=1, source_target_pairs={{0,8},{8,16},{16,24},{24,32},{32,40},{40,48},{48,56},{56,64},{64,7... | collective-permute-start | bytes 196616 | tf_op jit(solution)/shard_map/while/body/eval_jaxpr/ppermute | solution.py:15
  179.1 9.3 %collective-permute-start = (bf16[8,64,64]{2,1,0:T(8,128)(2,1)S(1)}, bf16[8,64,64]{2,1,0:T(8,128)(2,1)S(1)}, u32[]{:S(2)}, u32[]{:S(2)}) collective-permute-start(bf16[8,64,64]{2,1,0:T(8,128)(2,1)S(1)} %fusion.131), channel_id=1, source_target_pairs={{0,8},{8,16},{16,24},{24,32},{32,40},{40,48},{48,56},{56,64},{64,7... | collective-permute-start | bytes 196616 | tf_op jit(solution)/shard_map/while/body/eval_jaxpr/ppermute | solution.py:15
  257.6 30.8 %all-to-all-start.1 = ((bf16[8,128,448]{1,2,0:T(8,128)(2,1)}), bf16[8,128,448]{1,2,0:T(8,128)(2,1)S(1)}, u32[]{:S(2)}, u32[]{:S(2)}) async-start(bf16[8,128,448]{1,2,0:T(8,128)(2,1)} %stack.13), calls=%async_computation.2 | async-start | bytes 1835008 | tf_op jit(solution)/shard_map/all_to_all | solution.py:77
  261.9 236.1 %reduce-scatter.6.cloned.1.call-start = ((), (), s32[]{:S(2)}) async-start(), calls=%async_computation.7 | async-start | bytes 1032192 | tf_op jit(solution)/shard_map/reduce_scatter | solution.py:124
  301.7 6.9 collective-permute-start.1
  308.7 6.9 collective-permute-start.1
  322.7 7.8 %collective-permute-start.1 = (bf16[8,64,64]{2,1,0:T(8,128)(2,1)S(1)}, bf16[8,64,64]{2,1,0:T(8,128)(2,1)S(1)}, u32[]{:S(2)}, u32[]{:S(2)}) collective-permute-start(bf16[8,64,64]{2,1,0:T(8,128)(2,1)S(1)} %fusion.132), channel_id=1, source_target_pairs={{0,8},{8,16},{16,24},{24,32},{32,40},{40,48},{48,56},{56,64},{64,7... | collective-permute-start | bytes 196616 | tf_op jit(solution)/shard_map/while/body/eval_jaxpr/ppermute | solution.py:15
  330.7 9.0 %collective-permute-start.1 = (bf16[8,64,64]{2,1,0:T(8,128)(2,1)S(1)}, bf16[8,64,64]{2,1,0:T(8,128)(2,1)S(1)}, u32[]{:S(2)}, u32[]{:S(2)}) collective-permute-start(bf16[8,64,64]{2,1,0:T(8,128)(2,1)S(1)} %fusion.132), channel_id=1, source_target_pairs={{0,8},{8,16},{16,24},{24,32},{32,40},{40,48},{48,56},{56,64},{64,7... | collective-permute-start | bytes 196616 | tf_op jit(solution)/shard_map/while/body/eval_jaxpr/ppermute | solution.py:15
  339.8 9.6 %collective-permute-start.1 = (bf16[8,64,64]{2,1,0:T(8,128)(2,1)S(1)}, bf16[8,64,64]{2,1,0:T(8,128)(2,1)S(1)}, u32[]{:S(2)}, u32[]{:S(2)}) collective-permute-start(bf16[8,64,64]{2,1,0:T(8,128)(2,1)S(1)} %fusion.132), channel_id=1, source_target_pairs={{0,8},{8,16},{16,24},{24,32},{32,40},{40,48},{48,56},{56,64},{64,7... | collective-permute-start | bytes 196616 | tf_op jit(solution)/shard_map/while/body/eval_jaxpr/ppermute | solution.py:15
  349.6 10.3 %collective-permute-start.1 = (bf16[8,64,64]{2,1,0:T(8,128)(2,1)S(1)}, bf16[8,64,64]{2,1,0:T(8,128)(2,1)S(1)}, u32[]{:S(2)}, u32[]{:S(2)}) collective-permute-start(bf16[8,64,64]{2,1,0:T(8,128)(2,1)S(1)} %fusion.132), channel_id=1, source_target_pairs={{0,8},{8,16},{16,24},{24,32},{32,40},{40,48},{48,56},{56,64},{64,7... | collective-permute-start | bytes 196616 | tf_op jit(solution)/shard_map/while/body/eval_jaxpr/ppermute | solution.py:15
  360.0 9.0 %collective-permute-start.1 = (bf16[8,64,64]{2,1,0:T(8,128)(2,1)S(1)}, bf16[8,64,64]{2,1,0:T(8,128)(2,1)S(1)}, u32[]{:S(2)}, u32[]{:S(2)}) collective-permute-start(bf16[8,64,64]{2,1,0:T(8,128)(2,1)S(1)} %fusion.132), channel_id=1, source_target_pairs={{0,8},{8,16},{16,24},{24,32},{32,40},{40,48},{48,56},{56,64},{64,7... | collective-permute-start | bytes 196616 | tf_op jit(solution)/shard_map/while/body/eval_jaxpr/ppermute | solution.py:15
  369.2 8.8 %collective-permute-start.1 = (bf16[8,64,64]{2,1,0:T(8,128)(2,1)S(1)}, bf16[8,64,64]{2,1,0:T(8,128)(2,1)S(1)}, u32[]{:S(2)}, u32[]{:S(2)}) collective-permute-start(bf16[8,64,64]{2,1,0:T(8,128)(2,1)S(1)} %fusion.132), channel_id=1, source_target_pairs={{0,8},{8,16},{16,24},{24,32},{32,40},{40,48},{48,56},{56,64},{64,7... | collective-permute-start | bytes 196616 | tf_op jit(solution)/shard_map/while/body/eval_jaxpr/ppermute | solution.py:15
  378.2 9.0 %collective-permute-start.1 = (bf16[8,64,64]{2,1,0:T(8,128)(2,1)S(1)}, bf16[8,64,64]{2,1,0:T(8,128)(2,1)S(1)}, u32[]{:S(2)}, u32[]{:S(2)}) collective-permute-start(bf16[8,64,64]{2,1,0:T(8,128)(2,1)S(1)} %fusion.132), channel_id=1, source_target_pairs={{0,8},{8,16},{16,24},{24,32},{32,40},{40,48},{48,56},{56,64},{64,7... | collective-permute-start | bytes 196616 | tf_op jit(solution)/shard_map/while/body/eval_jaxpr/ppermute | solution.py:15
  387.3 9.0 %collective-permute-start.1 = (bf16[8,64,64]{2,1,0:T(8,128)(2,1)S(1)}, bf16[8,64,64]{2,1,0:T(8,128)(2,1)S(1)}, u32[]{:S(2)}, u32[]{:S(2)}) collective-permute-start(bf16[8,64,64]{2,1,0:T(8,128)(2,1)S(1)} %fusion.132), channel_id=1, source_target_pairs={{0,8},{8,16},{16,24},{24,32},{32,40},{40,48},{48,56},{56,64},{64,7... | collective-permute-start | bytes 196616 | tf_op jit(solution)/shard_map/while/body/eval_jaxpr/ppermute | solution.py:15
  396.4 9.0 %collective-permute-start.1 = (bf16[8,64,64]{2,1,0:T(8,128)(2,1)S(1)}, bf16[8,64,64]{2,1,0:T(8,128)(2,1)S(1)}, u32[]{:S(2)}, u32[]{:S(2)}) collective-permute-start(bf16[8,64,64]{2,1,0:T(8,128)(2,1)S(1)} %fusion.132), channel_id=1, source_target_pairs={{0,8},{8,16},{16,24},{24,32},{32,40},{40,48},{48,56},{56,64},{64,7... | collective-permute-start | bytes 196616 | tf_op jit(solution)/shard_map/while/body/eval_jaxpr/ppermute | solution.py:15
  405.6 9.2 %collective-permute-start.1 = (bf16[8,64,64]{2,1,0:T(8,128)(2,1)S(1)}, bf16[8,64,64]{2,1,0:T(8,128)(2,1)S(1)}, u32[]{:S(2)}, u32[]{:S(2)}) collective-permute-start(bf16[8,64,64]{2,1,0:T(8,128)(2,1)S(1)} %fusion.132), channel_id=1, source_target_pairs={{0,8},{8,16},{16,24},{24,32},{32,40},{40,48},{48,56},{56,64},{64,7... | collective-permute-start | bytes 196616 | tf_op jit(solution)/shard_map/while/body/eval_jaxpr/ppermute | solution.py:15
  414.9 9.3 %collective-permute-start.1 = (bf16[8,64,64]{2,1,0:T(8,128)(2,1)S(1)}, bf16[8,64,64]{2,1,0:T(8,128)(2,1)S(1)}, u32[]{:S(2)}, u32[]{:S(2)}) collective-permute-start(bf16[8,64,64]{2,1,0:T(8,128)(2,1)S(1)} %fusion.132), channel_id=1, source_target_pairs={{0,8},{8,16},{16,24},{24,32},{32,40},{40,48},{48,56},{56,64},{64,7... | collective-permute-start | bytes 196616 | tf_op jit(solution)/shard_map/while/body/eval_jaxpr/ppermute | solution.py:15
  424.4 9.3 %collective-permute-start.1 = (bf16[8,64,64]{2,1,0:T(8,128)(2,1)S(1)}, bf16[8,64,64]{2,1,0:T(8,128)(2,1)S(1)}, u32[]{:S(2)}, u32[]{:S(2)}) collective-permute-start(bf16[8,64,64]{2,1,0:T(8,128)(2,1)S(1)} %fusion.132), channel_id=1, source_target_pairs={{0,8},{8,16},{16,24},{24,32},{32,40},{40,48},{48,56},{56,64},{64,7... | collective-permute-start | bytes 196616 | tf_op jit(solution)/shard_map/while/body/eval_jaxpr/ppermute | solution.py:15
  502.3 30.8 %all-to-all-start.2 = ((bf16[8,128,448]{1,2,0:T(8,128)(2,1)}), bf16[8,128,448]{1,2,0:T(8,128)(2,1)S(1)}, u32[]{:S(2)}, u32[]{:S(2)}) async-start(bf16[8,128,448]{1,2,0:T(8,128)(2,1)} %stack.15), calls=%async_computation.4 | async-start | bytes 1835008 | tf_op jit(solution)/shard_map/all_to_all | solution.py:77
  506.6 236.1 %reduce-scatter.8.cloned.1.call-start = ((), (), s32[]{:S(2)}) async-start(), calls=%async_computation.8 | async-start | bytes 1032192 | tf_op jit(solution)/shard_map/reduce_scatter | solution.py:124
  567.4 7.9 %collective-permute-start.2 = (bf16[8,64,64]{2,1,0:T(8,128)(2,1)S(1)}, bf16[8,64,64]{2,1,0:T(8,128)(2,1)S(1)}, u32[]{:S(2)}, u32[]{:S(2)}) collective-permute-start(bf16[8,64,64]{2,1,0:T(8,128)(2,1)S(1)} %fusion.133), channel_id=1, source_target_pairs={{0,8},{8,16},{16,24},{24,32},{32,40},{40,48},{48,56},{56,64},{64,7... | collective-permute-start | bytes 196616 | tf_op jit(solution)/shard_map/while/body/eval_jaxpr/ppermute | solution.py:15
  575.4 9.0 %collective-permute-start.2 = (bf16[8,64,64]{2,1,0:T(8,128)(2,1)S(1)}, bf16[8,64,64]{2,1,0:T(8,128)(2,1)S(1)}, u32[]{:S(2)}, u32[]{:S(2)}) collective-permute-start(bf16[8,64,64]{2,1,0:T(8,128)(2,1)S(1)} %fusion.133), channel_id=1, source_target_pairs={{0,8},{8,16},{16,24},{24,32},{32,40},{40,48},{48,56},{56,64},{64,7... | collective-permute-start | bytes 196616 | tf_op jit(solution)/shard_map/while/body/eval_jaxpr/ppermute | solution.py:15
  584.6 9.6 %collective-permute-start.2 = (bf16[8,64,64]{2,1,0:T(8,128)(2,1)S(1)}, bf16[8,64,64]{2,1,0:T(8,128)(2,1)S(1)}, u32[]{:S(2)}, u32[]{:S(2)}) collective-permute-start(bf16[8,64,64]{2,1,0:T(8,128)(2,1)S(1)} %fusion.133), channel_id=1, source_target_pairs={{0,8},{8,16},{16,24},{24,32},{32,40},{40,48},{48,56},{56,64},{64,7... | collective-permute-start | bytes 196616 | tf_op jit(solution)/shard_map/while/body/eval_jaxpr/ppermute | solution.py:15
  594.3 10.3 %collective-permute-start.2 = (bf16[8,64,64]{2,1,0:T(8,128)(2,1)S(1)}, bf16[8,64,64]{2,1,0:T(8,128)(2,1)S(1)}, u32[]{:S(2)}, u32[]{:S(2)}) collective-permute-start(bf16[8,64,64]{2,1,0:T(8,128)(2,1)S(1)} %fusion.133), channel_id=1, source_target_pairs={{0,8},{8,16},{16,24},{24,32},{32,40},{40,48},{48,56},{56,64},{64,7... | collective-permute-start | bytes 196616 | tf_op jit(solution)/shard_map/while/body/eval_jaxpr/ppermute | solution.py:15
  604.8 9.1 %collective-permute-start.2 = (bf16[8,64,64]{2,1,0:T(8,128)(2,1)S(1)}, bf16[8,64,64]{2,1,0:T(8,128)(2,1)S(1)}, u32[]{:S(2)}, u32[]{:S(2)}) collective-permute-start(bf16[8,64,64]{2,1,0:T(8,128)(2,1)S(1)} %fusion.133), channel_id=1, source_target_pairs={{0,8},{8,16},{16,24},{24,32},{32,40},{40,48},{48,56},{56,64},{64,7... | collective-permute-start | bytes 196616 | tf_op jit(solution)/shard_map/while/body/eval_jaxpr/ppermute | solution.py:15
  614.0 8.8 %collective-permute-start.2 = (bf16[8,64,64]{2,1,0:T(8,128)(2,1)S(1)}, bf16[8,64,64]{2,1,0:T(8,128)(2,1)S(1)}, u32[]{:S(2)}, u32[]{:S(2)}) collective-permute-start(bf16[8,64,64]{2,1,0:T(8,128)(2,1)S(1)} %fusion.133), channel_id=1, source_target_pairs={{0,8},{8,16},{16,24},{24,32},{32,40},{40,48},{48,56},{56,64},{64,7... | collective-permute-start | bytes 196616 | tf_op jit(solution)/shard_map/while/body/eval_jaxpr/ppermute | solution.py:15
  622.9 9.0 %collective-permute-start.2 = (bf16[8,64,64]{2,1,0:T(8,128)(2,1)S(1)}, bf16[8,64,64]{2,1,0:T(8,128)(2,1)S(1)}, u32[]{:S(2)}, u32[]{:S(2)}) collective-permute-start(bf16[8,64,64]{2,1,0:T(8,128)(2,1)S(1)} %fusion.133), channel_id=1, source_target_pairs={{0,8},{8,16},{16,24},{24,32},{32,40},{40,48},{48,56},{56,64},{64,7... | collective-permute-start | bytes 196616 | tf_op jit(solution)/shard_map/while/body/eval_jaxpr/ppermute | solution.py:15
  632.1 9.0 %collective-permute-start.2 = (bf16[8,64,64]{2,1,0:T(8,128)(2,1)S(1)}, bf16[8,64,64]{2,1,0:T(8,128)(2,1)S(1)}, u32[]{:S(2)}, u32[]{:S(2)}) collective-permute-start(bf16[8,64,64]{2,1,0:T(8,128)(2,1)S(1)} %fusion.133), channel_id=1, source_target_pairs={{0,8},{8,16},{16,24},{24,32},{32,40},{40,48},{48,56},{56,64},{64,7... | collective-permute-start | bytes 196616 | tf_op jit(solution)/shard_map/while/body/eval_jaxpr/ppermute | solution.py:15
  641.2 9.0 %collective-permute-start.2 = (bf16[8,64,64]{2,1,0:T(8,128)(2,1)S(1)}, bf16[8,64,64]{2,1,0:T(8,128)(2,1)S(1)}, u32[]{:S(2)}, u32[]{:S(2)}) collective-permute-start(bf16[8,64,64]{2,1,0:T(8,128)(2,1)S(1)} %fusion.133), channel_id=1, source_target_pairs={{0,8},{8,16},{16,24},{24,32},{32,40},{40,48},{48,56},{56,64},{64,7... | collective-permute-start | bytes 196616 | tf_op jit(solution)/shard_map/while/body/eval_jaxpr/ppermute | solution.py:15
  650.3 9.2 %collective-permute-start.2 = (bf16[8,64,64]{2,1,0:T(8,128)(2,1)S(1)}, bf16[8,64,64]{2,1,0:T(8,128)(2,1)S(1)}, u32[]{:S(2)}, u32[]{:S(2)}) collective-permute-start(bf16[8,64,64]{2,1,0:T(8,128)(2,1)S(1)} %fusion.133), channel_id=1, source_target_pairs={{0,8},{8,16},{16,24},{24,32},{32,40},{40,48},{48,56},{56,64},{64,7... | collective-permute-start | bytes 196616 | tf_op jit(solution)/shard_map/while/body/eval_jaxpr/ppermute | solution.py:15
  659.7 9.3 %collective-permute-start.2 = (bf16[8,64,64]{2,1,0:T(8,128)(2,1)S(1)}, bf16[8,64,64]{2,1,0:T(8,128)(2,1)S(1)}, u32[]{:S(2)}, u32[]{:S(2)}) collective-permute-start(bf16[8,64,64]{2,1,0:T(8,128)(2,1)S(1)} %fusion.133), channel_id=1, source_target_pairs={{0,8},{8,16},{16,24},{24,32},{32,40},{40,48},{48,56},{56,64},{64,7... | collective-permute-start | bytes 196616 | tf_op jit(solution)/shard_map/while/body/eval_jaxpr/ppermute | solution.py:15
  669.1 9.3 %collective-permute-start.2 = (bf16[8,64,64]{2,1,0:T(8,128)(2,1)S(1)}, bf16[8,64,64]{2,1,0:T(8,128)(2,1)S(1)}, u32[]{:S(2)}, u32[]{:S(2)}) collective-permute-start(bf16[8,64,64]{2,1,0:T(8,128)(2,1)S(1)} %fusion.133), channel_id=1, source_target_pairs={{0,8},{8,16},{16,24},{24,32},{32,40},{40,48},{48,56},{56,64},{64,7... | collective-permute-start | bytes 196616 | tf_op jit(solution)/shard_map/while/body/eval_jaxpr/ppermute | solution.py:15
  (28 other events, 526.7 us)
Sparse Core Ops, SparseCore 0:
  209.6 43.6 reduce-scatter.3
  454.3 43.6 reduce-scatter.5
  699.0 43.6 reduce-scatter.7
